TPU v7x, 32 devices: a whole 2x2x4 slice. The times are simulated.
32 devices in a mesh: dp: 16 (over z, y, core), mp: 2 (over x).
Axes of the slice: x: 2, y: 2, z: 4, core: 2. Of those that a mesh axis runs over, the one named last changes fastest.
Arguments:
- tokens: bfloat16 [16, 448, 768], P('dp'), may hold values from -6 to 6
- frames: bfloat16 [16, 1500, 768], P('dp'), may hold values from -6 to 6
- lengths: int32 [16], P('dp'), may hold values from 1 to 448, as said below
- out_cot: bfloat16 [16, 448, 768], P('dp'), may hold values from -6 to 6
- self_query_key_value: bfloat16 [768, 3, 768], P(None, None, 'mp'), may hold values from -0.21875 to 0.21875
- self_qv_bias: float32 [2, 768], P(None, 'mp'), may hold values from -1.75 to 1.75
- self_output_weight: bfloat16 [768, 768], P('mp'), may hold values from -0.875 to 0.875
- cross_query_weight: bfloat16 [768, 768], P(None, 'mp'), may hold values from -0.21875 to 0.21875
- cross_kv: bfloat16 [768, 2, 768], P(None, None, 'mp'), may hold values from -0.21875 to 0.21875
- cross_bias: float32 [2, 768], P(None, 'mp'), may hold values from -1.75 to 1.75
- cross_output_weight: bfloat16 [768, 768], P('mp'), may hold values from -1.25 to 1.25
- first_dense_weight: bfloat16 [768, 3072], P(None, 'mp'), may hold values from -0.21875 to 0.21875
- first_dense_bias: float32 [3072], P('mp'), may hold values from -1.75 to 1.75
- second_dense_weight: bfloat16 [3072, 768], P('mp'), may hold values from -0.109375 to 0.109375
- out_biases: float32 [3, 768], replicated, may hold values from -1.75 to 1.75
- norm_gains: float32 [4, 768], replicated, may hold values from 0.25 to 1.75
- norm_biases: float32 [4, 768], replicated, may hold values from -1.75 to 1.75
Outputs:
- out: bfloat16 [16, 448, 768], P('dp')
- tokens_grad: float32 [16, 448, 768], P('dp')
- frames_grad: float32 [16, 1500, 768], P('dp', None, 'mp')
- self_qkv_grad: float32 [768, 3, 768], P('dp', None, 'mp')
- self_qv_bias_grad: float32 [2, 768], P(None, 'mp')
- self_out_grad: float32 [768, 768], P('mp', 'dp')
- cross_q_grad: float32 [768, 768], P('dp', 'mp')
- cross_kv_grad: float32 [768, 2, 768], P('dp', None, 'mp')
- cross_bias_grad: float32 [2, 768], P(None, 'mp')
- cross_out_grad: float32 [768, 768], P('mp', 'dp')
- fc1_grad: float32 [768, 3072], P('dp', 'mp')
- fc1_bias_grad: float32 [3072], P('mp')
- second_dense_gradient: float32 [3072, 768], P('mp', 'dp')
- out_biases_grad: float32 [3, 768], replicated
- norm_gains_grad: float32 [4, 768], replicated
- norm_biases_grad: float32 [4, 768], replicated
Inputs may be any that keep to these rules, and one draw needn't show every extreme that they name: `lengths`: each transcript has at least one token; some transcript fills all 448 slots.
All inputs are finite; a program needn't handle non-finite values.
Results may differ from a plain program's by a relative error of at most 0.024.
Values sent between devices are 32-bit elements; how exact they have to be, the bound alone decides.
No kernel may reach another device: no remote copies, remote signals or barrier semaphores. Data moves between devices by JAX's collectives and lax.ppermute only.
A program may use at most 192 MiB of HBM per device.

v0:
```python
from functools import partial

import jax
import jax.numpy as jnp
from jax import lax
from jax.sharding import PartitionSpec as P

HEAD_DIM = 64


def norm_rows(stream, norm_gain, norm_shift):
    centred = stream - jnp.mean(stream, axis=-1, keepdims=True)
    spread = jnp.mean(centred * centred, axis=-1, keepdims=True)
    return centred * lax.rsqrt(spread + 1e-05) * norm_gain + norm_shift


def split_heads(flat_rows):
    return flat_rows.reshape(flat_rows.shape[0], flat_rows.shape[1], -1, HEAD_DIM)


def join_heads(headed):
    return headed.reshape(headed.shape[0], headed.shape[1], -1)


def score_block(query_rows, key_rows, key_mask):
    scores = jnp.einsum("sqhd,skhd->shqk", query_rows, key_rows, preferred_element_type=jnp.float32)
    if key_mask is not None:
        scores = jnp.where(key_mask, scores, -1e30)
    return scores


def attend_forward(query_rows, key_rows, value_rows, key_mask):
    scores = score_block(query_rows, key_rows, key_mask)
    highest = jnp.max(scores, axis=-1, keepdims=True)
    log_total = highest + jnp.log(jnp.sum(jnp.exp(scores - highest), axis=-1, keepdims=True))
    weights = jnp.exp(scores - log_total).astype(jnp.bfloat16)
    mixed_heads = jnp.einsum(
        "shqk,skhd->sqhd", weights, value_rows, preferred_element_type=jnp.float32
    )
    return (join_heads(mixed_heads).astype(jnp.bfloat16), log_total)


def attend_backward(query_rows, key_rows, value_rows, key_mask, log_total, grad_mixed):
    grad_heads = split_heads(grad_mixed)
    softmax_out = jnp.exp(score_block(query_rows, key_rows, key_mask) - log_total)
    weights = softmax_out.astype(jnp.bfloat16)
    grad_probs = jnp.einsum(
        "sqhd,skhd->shqk", grad_heads, value_rows, preferred_element_type=jnp.float32
    )
    inner_sum = jnp.sum(softmax_out * grad_probs, axis=-1, keepdims=True)
    grad_scores = (softmax_out * (grad_probs - inner_sum)).astype(jnp.bfloat16)
    grad_queries = jnp.einsum(
        "shqk,skhd->sqhd", grad_scores, key_rows, preferred_element_type=jnp.float32
    )
    grad_keys = jnp.einsum(
        "shqk,sqhd->skhd", grad_scores, query_rows, preferred_element_type=jnp.float32
    )
    grad_values = jnp.einsum(
        "shqk,sqhd->skhd", weights, grad_heads, preferred_element_type=jnp.float32
    )
    return (
        join_heads(grad_queries).astype(jnp.bfloat16),
        join_heads(grad_keys).astype(jnp.bfloat16),
        join_heads(grad_values).astype(jnp.bfloat16),
    )


def row_total(matrix_rows):
    return jnp.sum(matrix_rows, axis=(0, 1), dtype=jnp.float32)


def on_device(
    tokens,
    frames,
    lengths,
    out_cot,
    self_query_key_value,
    self_qv_bias,
    self_output_weight,
    cross_query_weight,
    cross_kv,
    cross_bias,
    cross_output_weight,
    first_dense_weight,
    first_dense_bias,
    second_dense_weight,
    out_biases,
    norm_gains,
    norm_biases,
):
    seq_count, slot_len, model_width = tokens.shape
    positions = jnp.arange(slot_len, dtype=jnp.int32)
    valid = (positions[None, :] < lengths[:, None]).astype(jnp.float32)[:, :, None]
    causal = positions[None, :] <= positions[:, None]
    key_mask = (causal[None] & (positions[None, None, :] < lengths[:, None, None]))[:, None]
    stream_zero = tokens.astype(jnp.float32)
    normed_one, pull_one = jax.vjp(norm_rows, stream_zero, norm_gains[0], norm_biases[0])
    first_input = normed_one.astype(jnp.bfloat16)
    merged_heads = jnp.einsum(
        "nef,fgt->negt", first_input, self_query_key_value, preferred_element_type=jnp.float32
    )
    queries_self = split_heads(
        ((merged_heads[:, :, 0] + self_qv_bias[0]) * 0.125).astype(jnp.bfloat16)
    )
    keys_self = split_heads(merged_heads[:, :, 1].astype(jnp.bfloat16))
    values_self = split_heads((merged_heads[:, :, 2] + self_qv_bias[1]).astype(jnp.bfloat16))
    self_mixture, lse_self = attend_forward(queries_self, keys_self, values_self, key_mask)
    self_portion = jnp.einsum(
        "zhn,nq->zhq", self_mixture, self_output_weight, preferred_element_type=jnp.float32
    )
    stream_one = stream_zero + lax.psum(self_portion, "mp") + out_biases[0]
    normed_two, pull_two = jax.vjp(norm_rows, stream_one, norm_gains[1], norm_biases[1])
    second_input = normed_two.astype(jnp.bfloat16)
    query_projected = jnp.einsum(
        "kqe,ez->kqz", second_input, cross_query_weight, preferred_element_type=jnp.float32
    )
    queries_cross = split_heads(((query_projected + cross_bias[0]) * 0.125).astype(jnp.bfloat16))
    frame_pair = jnp.einsum("sfd,dkc->sfkc", frames, cross_kv, preferred_element_type=jnp.float32)
    keys_cross = split_heads(frame_pair[:, :, 0].astype(jnp.bfloat16))
    values_cross = split_heads((frame_pair[:, :, 1] + cross_bias[1]).astype(jnp.bfloat16))
    cross_mixture, lse_cross = attend_forward(queries_cross, keys_cross, values_cross, None)
    part_cross = jnp.einsum(
        "zhn,nq->zhq", cross_mixture, cross_output_weight, preferred_element_type=jnp.float32
    )
    stream_two = stream_one + lax.psum(part_cross, "mp") + out_biases[1]
    normed_three, pull_three = jax.vjp(norm_rows, stream_two, norm_gains[2], norm_biases[2])
    third_input = normed_three.astype(jnp.bfloat16)
    hidden = (
        jnp.einsum(
            "gwz,zj->gwj", third_input, first_dense_weight, preferred_element_type=jnp.float32
        )
        + first_dense_bias
    )
    active, gelu_pull = jax.vjp(partial(jax.nn.gelu, approximate=False), hidden)
    active_reduced = active.astype(jnp.bfloat16)
    dense_portion = jnp.einsum(
        "twe,eh->twh", active_reduced, second_dense_weight, preferred_element_type=jnp.float32
    )
    stream_three = stream_two + lax.psum(dense_portion, "mp") + out_biases[2]
    final_norm, pull_four = jax.vjp(norm_rows, stream_three, norm_gains[3], norm_biases[3])
    output = (final_norm * valid).astype(jnp.bfloat16)
    grad_three, gain_four, shift_four = pull_four(out_cot.astype(jnp.float32) * valid)
    reduced_third = grad_three.astype(jnp.bfloat16)
    second_dense_gradient = jnp.einsum(
        "jvb,jvy->by", active_reduced, reduced_third, preferred_element_type=jnp.float32
    )
    active_gradient = jnp.einsum(
        "vcy,wy->vcw", reduced_third, second_dense_weight, preferred_element_type=jnp.float32
    )
    reduced_hidden = gelu_pull(active_gradient)[0].astype(jnp.bfloat16)
    fc1_grad = jnp.einsum(
        "ney,nev->yv", third_input, reduced_hidden, preferred_element_type=jnp.float32
    )
    fc1_bias_grad = row_total(reduced_hidden)
    reverse_third = jnp.einsum(
        "beq,nq->ben", reduced_hidden, first_dense_weight, preferred_element_type=jnp.float32
    )
    grad_normed_three = lax.psum(reverse_third, "mp")
    grad_part_two, gain_three, shift_three = pull_three(grad_normed_three)
    grad_two = grad_three + grad_part_two
    reduced_second = grad_two.astype(jnp.bfloat16)
    cross_out_grad = jnp.einsum(
        "vpe,vph->eh", cross_mixture, reduced_second, preferred_element_type=jnp.float32
    )
    grad_mixed_cross = jnp.einsum(
        "fgv,xv->fgx", reduced_second, cross_output_weight, preferred_element_type=jnp.float32
    ).astype(jnp.bfloat16)
    grad_qc, grad_kc, grad_vc = attend_backward(
        queries_cross, keys_cross, values_cross, None, lse_cross, grad_mixed_cross
    )
    reduced_cross_query = grad_qc * 0.125
    low_frame_pair = jnp.stack([grad_kc, grad_vc], axis=2)
    cross_q_grad = jnp.einsum(
        "ufk,ufn->kn", second_input, reduced_cross_query, preferred_element_type=jnp.float32
    )
    cross_kv_grad = jnp.einsum(
        "sfd,sfkc->dkc", frames, low_frame_pair, preferred_element_type=jnp.float32
    )
    cross_bias_grad = jnp.stack([row_total(reduced_cross_query), row_total(grad_vc)])
    frame_terms = jnp.einsum(
        "sfkc,dkc->sfd", low_frame_pair, cross_kv, preferred_element_type=jnp.float32
    )
    frames_grad = lax.psum_scatter(frame_terms, "mp", scatter_dimension=2, tiled=True)
    back_two = jnp.einsum(
        "qkg,mg->qkm", reduced_cross_query, cross_query_weight, preferred_element_type=jnp.float32
    )
    grad_normed_two = lax.psum(back_two, "mp")
    grad_part_one, gain_two, shift_two = pull_two(grad_normed_two)
    grad_one = grad_two + grad_part_one
    reduced_first = grad_one.astype(jnp.bfloat16)
    self_out_grad = jnp.einsum(
        "vpe,vph->eh", self_mixture, reduced_first, preferred_element_type=jnp.float32
    )
    grad_mixed_self = jnp.einsum(
        "fgv,xv->fgx", reduced_first, self_output_weight, preferred_element_type=jnp.float32
    ).astype(jnp.bfloat16)
    grad_qs, grad_ks, grad_vs = attend_backward(
        queries_self, keys_self, values_self, key_mask, lse_self, grad_mixed_self
    )
    low_query_self = grad_qs * 0.125
    reduced_merged = jnp.stack([low_query_self, grad_ks, grad_vs], axis=2)
    self_qkv_grad = jnp.einsum(
        "gpq,gpnm->qnm", first_input, reduced_merged, preferred_element_type=jnp.float32
    )
    self_qv_bias_grad = jnp.stack([row_total(low_query_self), row_total(grad_vs)])
    reverse_first = jnp.einsum(
        "mqrn,frn->mqf", reduced_merged, self_query_key_value, preferred_element_type=jnp.float32
    )
    grad_normed_one = lax.psum(reverse_first, "mp")
    grad_part_zero, gain_one, shift_one = pull_one(grad_normed_one)
    tokens_grad = grad_one + grad_part_zero
    (
        self_qkv_grad,
        self_out_grad,
        cross_q_grad,
        cross_kv_grad,
        cross_out_grad,
        fc1_grad,
        second_dense_gradient,
    ) = (
        lax.psum_scatter(self_qkv_grad, "dp", scatter_dimension=0, tiled=True),
        lax.psum_scatter(self_out_grad, "dp", scatter_dimension=1, tiled=True),
        lax.psum_scatter(cross_q_grad, "dp", scatter_dimension=0, tiled=True),
        lax.psum_scatter(cross_kv_grad, "dp", scatter_dimension=0, tiled=True),
        lax.psum_scatter(cross_out_grad, "dp", scatter_dimension=1, tiled=True),
        lax.psum_scatter(fc1_grad, "dp", scatter_dimension=0, tiled=True),
        lax.psum_scatter(second_dense_gradient, "dp", scatter_dimension=1, tiled=True),
    )
    out_biases_grad = jnp.stack([row_total(grad_one), row_total(grad_two), row_total(grad_three)])
    norm_gains_grad = jnp.stack([gain_one, gain_two, gain_three, gain_four])
    norm_biases_grad = jnp.stack([shift_one, shift_two, shift_three, shift_four])
    (
        self_qv_bias_grad,
        cross_bias_grad,
        fc1_bias_grad,
        out_biases_grad,
        norm_gains_grad,
        norm_biases_grad,
    ) = lax.psum(
        (
            self_qv_bias_grad,
            cross_bias_grad,
            fc1_bias_grad,
            out_biases_grad,
            norm_gains_grad,
            norm_biases_grad,
        ),
        "dp",
    )
    return (
        output,
        tokens_grad,
        frames_grad,
        self_qkv_grad,
        self_qv_bias_grad,
        self_out_grad,
        cross_q_grad,
        cross_kv_grad,
        cross_bias_grad,
        cross_out_grad,
        fc1_grad,
        fc1_bias_grad,
        second_dense_gradient,
        out_biases_grad,
        norm_gains_grad,
        norm_biases_grad,
    )


def solution(mesh):
    in_specs = (
        P("dp", None, None),
        P("dp", None, None),
        P("dp"),
        P("dp", None, None),
        P(None, None, "mp"),
        P(None, "mp"),
        P("mp", None),
        P(None, "mp"),
        P(None, None, "mp"),
        P(None, "mp"),
        P("mp", None),
        P(None, "mp"),
        P("mp"),
        P("mp", None),
        P(),
        P(),
        P(),
    )
    out_specs = (
        P("dp", None, None),
        P("dp", None, None),
        P("dp", None, "mp"),
        P("dp", None, "mp"),
        P(None, "mp"),
        P("mp", "dp"),
        P("dp", "mp"),
        P("dp", None, "mp"),
        P(None, "mp"),
        P("mp", "dp"),
        P("dp", "mp"),
        P("mp"),
        P("mp", "dp"),
        P(),
        P(),
        P(),
    )
    return jax.shard_map(
        on_device, mesh=mesh, in_specs=in_specs, out_specs=out_specs, check_vma=False
    )
```

profile of v0, /device:TPU:0, one launch (start us, length us, event | category | flops | bytes accessed | tf_op | source)
XLA Modules:
  0.0 1000.9 jit_solution(4411748237045163910)
XLA Ops:
  10.9 2.7 convolution_bitcast_fusion.2
  16.5 1.9 copy.82
  18.4 2.3 copy.80
  20.7 2.3 copy.81
  22.9 2.4 select_reduce_fusion
  29.9 1.6 convolution_bitcast_fusion.6
  31.8 4.0 convolution_bitcast_fusion.1
  37.0 1.5 slice.85
  38.6 2.5 copy.87
  41.1 3.1 copy.85
  44.2 37.4 %all-reduce.10.cloned.1.call-done = f32[1,448,768]{2,1,0:T(8,128)} async-done(((f32[1,448,768]{2,1,0:T(8,128)}), f32[1,448,768]{2,1,0:T(8,128)}) %all-reduce.10.cloned.1.call-update) | async-done | bytes 1376272 | tf_op jit(solution)/shard_map/psum | solution.py:111
  81.6 1.6 fusion.95
  86.4 1.9 copy.86
  88.3 9.4 fusion.98
  97.7 8.1 exponential_reduce_fusion
  105.8 9.0 fusion.32
  115.5 1.6 convolution_bitcast_fusion.5
  117.6 46.9 %all-reduce.12.cloned.1.call-done = f32[1,448,768]{2,1,0:T(8,128)} async-done(((f32[1,448,768]{2,1,0:T(8,128)}), f32[1,448,768]{2,1,0:T(8,128)}) %all-reduce.12.cloned.1.call-update) | async-done | bytes 1376272 | tf_op jit(solution)/shard_map/psum | solution.py:125
  164.6 2.0 fusion.94
  167.3 8.4 multiply_convert_fusion.2
  176.8 2.3 convolution_bitcast_fusion.8
  179.2 47.3 %all-reduce.14.cloned.1.call-done = f32[1,448,768]{2,1,0:T(8,128)} async-done(((f32[1,448,768]{2,1,0:T(8,128)}), f32[1,448,768]{2,1,0:T(8,128)}) %all-reduce.14.cloned.1.call-update) | async-done | bytes 1376272 | tf_op jit(solution)/shard_map/psum | solution.py:139
  226.5 2.1 fusion.92
  230.5 1.6 fusion.91
  232.5 2.0 convert_reduce_fusion
  235.7 2.4 convolution_bitcast_fusion.7
  238.3 47.1 %all-reduce.16.cloned.1.call-done = f32[1,448,768]{2,1,0:T(8,128)} async-done(((f32[1,448,768]{2,1,0:T(8,128)}), f32[1,448,768]{2,1,0:T(8,128)}) %all-reduce.16.cloned.1.call-update) | async-done | bytes 1376272 | tf_op jit(solution)/shard_map/psum | solution.py:158
  285.4 2.0 multiply_reduce_fusion.3
  290.6 11.6 %multiply_reduce_fusion = (f32[6,448]{1,0:T(8,128)S(1)}, f32[6,448,1500]{2,1,0:T(8,128)}) fusion(f32[6,448,1500]{2,1,0:T(8,128)} %get-tuple-element.123, f32[6,448]{1,0:T(8,128)S(1)} %log_add_fusion, bf16[448,6,64]{0,2,1:T(8,128)(2,1)S(1)} %bitcast.175, f32[1500,6,64]{0,2,1:T(8,128)} %bitcast.164, f32[6,64]{1,0:T(8,128)S(1)} %add.268), kind=kOutput, calls=%fused_computation.1 | convolution fusion | flops 529341312 | bytes 34927104 | tf_op jit(solution)/shard_map/sqhd,skhd->shqk/dot_general | solution.py:47
  302.2 11.7 %multiply_convert_fusion = bf16[6,448,1500]{2,1,0:T(8,128)(2,1)S(1)} fusion(f32[6,448,1500]{2,1,0:T(8,128)} %get-tuple-element.126, f32[6,448,1500]{2,1,0:T(8,128)} %get-tuple-element.123, f32[6,448]{1,0:T(8,128)S(1)} %get-tuple-element.125, f32[6,448]{1,0:T(8,128)S(1)} %log_add_fusion), kind=kLoop, calls=%fused_computation | loop fusion | flops 16128000 | bytes 40341504 | tf_op jit(solution)/shard_map/convert_element_type | solution.py:51
  313.9 2.5 convert_reduce_fusion.3
  317.1 1.7 convolution_bitcast_fusion.4
  318.9 8.7 convert_reduce_fusion.1
  329.0 4.9 convolution_convert_fusion.1
  335.4 4.4 fusion.18
  339.8 3.1 copy.99
  343.2 23.0 %all-reduce.18.cloned.1.call-done = f32[1,448,768]{2,1,0:T(8,128)} async-done(((f32[1,448,768]{2,1,0:T(8,128)}), f32[1,448,768]{2,1,0:T(8,128)}) %all-reduce.18.cloned.1.call-update) | async-done | bytes 1376272 | tf_op jit(solution)/shard_map/psum | solution.py:187
  366.2 2.0 multiply_reduce_fusion.4
  371.9 1.9 copy.89
  373.8 5.0 multiply_reduce_fusion.1
  378.9 3.2 multiply_convert_fusion.1
  383.9 2.6 convert_reduce_fusion.5
  387.4 2.8 convolution_convert_fusion.3
  391.2 3.9 convolution_bitcast_fusion.3
  396.3 5.5 convolution_bitcast_fusion
  403.3 1.6 fusion.48
  405.0 2.8 fusion.99
  408.2 3.1 fusion.45
  411.4 5.1 fusion.83
  417.8 5.0 fusion.74
  423.9 3.1 fusion.52
  429.1 40.2 %all-reduce.22.cloned.1.call-done = f32[768,2,384]{2,1,0:T(2,128)} async-done(((f32[768,2,384]{2,1,0:T(2,128)}), f32[768,2,384]{2,1,0:T(2,128)}) %all-reduce.22.cloned.1.call-update) | async-done | bytes 2359312
  469.3 1.6 constant_dynamic-slice_fusion
  471.1 46.9 %all-reduce.20.cloned.1.call-done = f32[1,448,768]{2,1,0:T(8,128)} async-done(((f32[1,448,768]{2,1,0:T(8,128)}), f32[1,448,768]{2,1,0:T(8,128)}) %all-reduce.20.cloned.1.call-update) | async-done | bytes 1376272 | tf_op jit(solution)/shard_map/psum | solution.py:209
  518.0 1.9 fusion.86
  520.7 62.0 %all-reduce.1 = (f32[2,384]{1,0:T(2,128)}, f32[2,384]{1,0:T(2,128)}, f32[1536]{0:T(1024)}, f32[3,768]{1,0:T(4,128)}, f32[4,768]{1,0:T(4,128)}, /*index=5*/f32[4,768]{1,0:T(4,128)}) all-reduce(f32[2,384]{1,0:T(2,128)S(1)} %pad_maximum_fusion.3, f32[2,384]{1,0:T(2,128)S(1)} %pad_maximum_fusion.4, ...), channel_id=1, replica_groups=mesh['dp'=16,'mp'=2] {'dp'}, use_global_device_ids=true, to_apply=%region_32.33 | all-reduce | flops 11520 | bytes 92160 | tf_op jit(solution)/shard_map/psum | solution.py:239
  582.6 3.5 add_add_fusion.4
  586.1 6.4 copy.100
  592.5 49.1 %reduce-scatter.16.cloned.1.call-done = f32[384,48]{0,1:T(8,128)} async-done(((f32[384,768]{0,1:T(8,128)}), f32[384,48]{0,1:T(8,128)}) %reduce-scatter.16.cloned.1.call-update) | async-done | bytes 73744 | tf_op jit(solution)/shard_map/reduce_scatter | solution.py:225
  641.6 61.1 %reduce-scatter.14.cloned.1.call-done = f32[48,384]{1,0:T(8,128)} async-done(((f32[768,384]{1,0:T(8,128)}), f32[48,384]{1,0:T(8,128)}) %reduce-scatter.14.cloned.1.call-update) | async-done | bytes 73744 | tf_op jit(solution)/shard_map/reduce_scatter | solution.py:223
  702.7 61.3 %reduce-scatter.12.cloned.1.call-done = f32[384,48]{0,1:T(8,128)} async-done(((f32[384,768]{0,1:T(8,128)}), f32[384,48]{0,1:T(8,128)}) %reduce-scatter.12.cloned.1.call-update) | async-done | bytes 73744 | tf_op jit(solution)/shard_map/reduce_scatter | solution.py:222
  764.0 78.9 %reduce-scatter.18.cloned.1.call-done = f32[48,1536]{1,0:T(8,128)} async-done(((f32[768,1536]{1,0:T(8,128)}), f32[48,1536]{1,0:T(8,128)}) %reduce-scatter.18.cloned.1.call-update) | async-done | bytes 294928 | tf_op jit(solution)/shard_map/reduce_scatter | solution.py:226
  842.9 79.5 %reduce-scatter.20.cloned.1.call-done = f32[1536,48]{0,1:T(8,128)} async-done(((f32[1536,768]{0,1:T(8,128)}), f32[1536,48]{0,1:T(8,128)}) %reduce-scatter.20.cloned.1.call-update) | async-done | bytes 294928 | tf_op jit(solution)/shard_map/reduce_scatter | solution.py:227
  922.5 71.5 %reduce-scatter.10.cloned.1.call-done = f32[48,3,384]{2,0,1:T(8,128)} async-done(((f32[768,3,384]{2,0,1:T(8,128)}), f32[48,3,384]{2,0,1:T(8,128)}) %reduce-scatter.10.cloned.1.call-update) | async-done | bytes 221200 | tf_op jit(solution)/shard_map/reduce_scatter | solution.py:221
  (248 shorter events, 44.0 us)
Async XLA Ops:
  7.2 159.7 %copy-start = (bf16[768,1536]{1,0:T(8,128)(2,1)S(1)}, bf16[768,1536]{1,0:T(8,128)(2,1)}, u32[]{:S(2)}) copy-start(bf16[768,1536]{1,0:T(8,128)(2,1)} %param.28) | copy-start | bytes 7077892
  7.2 3.7 copy-start.9
  7.2 3.6 copy-start.54
  7.2 3.6 copy-start.55
  7.2 74.4 %all-reduce.10.cloned.1.call-start = ((), (), s32[]{:S(2)}) async-start(), calls=%async_computation.7 | async-start | bytes 2752512 | tf_op jit(solution)/shard_map/psum | solution.py:111
  8.7 4.9 copy-start.48
  10.8 2.8 copy-start.52
  10.9 2.7 copy-start.46
  10.9 2.7 copy-start.57
  14.4 1.8 copy-start.59
  25.3 2.5 copy-start.2
  25.3 2.4 copy-start.16
  27.8 2.1 copy-start.36
  31.6 133.0 %all-reduce.12.cloned.1.call-start = ((), (), s32[]{:S(2)}) async-start(), calls=%async_computation.8 | async-start | bytes 2752512 | tf_op jit(solution)/shard_map/psum | solution.py:125
  37.0 1.5 copy-start.60
  41.1 3.1 copy-start.56
  83.5 1.6 copy-start.41
  105.8 9.7 copy-start.34
  117.2 109.3 %all-reduce.14.cloned.1.call-start = ((), (), s32[]{:S(2)}) async-start(), calls=%async_computation.9 | async-start | bytes 2752512 | tf_op jit(solution)/shard_map/psum | solution.py:139
  166.5 9.1 copy-start.6
  167.3 9.6 copy-start.61
  179.2 106.3 %all-reduce.16.cloned.1.call-start = ((), (), s32[]{:S(2)}) async-start(), calls=%async_computation.10 | async-start | bytes 2752512 | tf_op jit(solution)/shard_map/psum | solution.py:158
  226.5 5.6 copy-start.68
  229.7 2.3 copy-start.67
  230.5 2.1 copy-start.62
  232.1 2.5 copy-start.20
  238.0 47.4 %copy-start.7 = (f32[1,448,768]{2,1,0:T(8,128)S(1)}, f32[1,448,768]{2,1,0:T(8,128)}, u32[]{:S(2)}) copy-start(f32[1,448,768]{2,1,0:T(8,128)} %copy-done.6) | copy-start | bytes 4128772
  238.1 128.1 %all-reduce.18.cloned.1.call-start = ((), (), s32[]{:S(2)}) async-start(), calls=%async_computation.11 | async-start | bytes 2752512 | tf_op jit(solution)/shard_map/psum | solution.py:187
  285.4 2.0 copy-start.24
  287.5 1.3 copy-start.21
  289.1 1.5 copy-start.11
  302.2 11.7 %copy-start.14 = (bf16[1,1500,1,384]{1,3,2,0:T(8,128)(2,1)S(1)}, bf16[1,1500,1,384]{1,3,2,0:T(8,128)(2,1)}, u32[]{:S(2)}) copy-start(bf16[1,1500,1,384]{1,3,2,0:T(8,128)(2,1)} %copy.87) | copy-start | bytes 3456004
  313.9 3.2 copy-start.3
  313.9 3.2 copy-start.42
  317.1 1.7 copy-start.25
  318.8 150.5 %all-reduce.22.cloned.1.call-start = ((), (), s32[]{:S(2)}) async-start(), calls=%async_computation.20 | async-start | bytes 4718592
  327.6 1.4 copy-start.19
  342.9 23.3 %copy-start.5 = (f32[1,448,768]{2,1,0:T(8,128)S(1)}, f32[1,448,768]{2,1,0:T(8,128)}, u32[]{:S(2)}) copy-start(f32[1,448,768]{2,1,0:T(8,128)} %copy-done.4) | copy-start | bytes 4128772
  342.9 175.1 %all-reduce.20.cloned.1.call-start = ((), (), s32[]{:S(2)}) async-start(), calls=%async_computation.12 | async-start | bytes 2752512 | tf_op jit(solution)/shard_map/psum | solution.py:209
  366.2 2.0 copy-start.23
  368.2 1.3 copy-start.12
  369.8 4.0 copy-start.10
  370.6 3.2 copy-start.17
  373.8 5.1 slice-start
  373.8 5.1 slice-start.1
  378.9 3.3 copy-start.38
  382.2 1.7 copy-start.29
  383.9 3.5 copy-start.18
  391.2 4.0 copy-start.40
  395.1 191.1 %reduce-scatter.8.cloned.1.call-start = ((), (), s32[]{:S(2)}) async-start(), calls=%async_computation.13 | async-start | bytes 6930432 | tf_op jit(solution)/shard_map/reduce_scatter | solution.py:183
  401.8 1.4 copy-start.31
  401.9 3.1 copy-start.26
  401.9 239.7 %reduce-scatter.16.cloned.1.call-start = ((), (), s32[]{:S(2)}) async-start(), calls=%async_computation.17 | async-start | bytes 1253376 | tf_op jit(solution)/shard_map/reduce_scatter | solution.py:225
  404.9 3.2 copy-start.28
  404.9 297.7 %reduce-scatter.14.cloned.1.call-start = ((), (), s32[]{:S(2)}) async-start(), calls=%async_computation.16 | async-start | bytes 1253376 | tf_op jit(solution)/shard_map/reduce_scatter | solution.py:223
  407.9 3.5 copy-start.8
  407.9 356.2 %reduce-scatter.12.cloned.1.call-start = ((), (), s32[]{:S(2)}) async-start(), calls=%async_computation.15 | async-start | bytes 1253376 | tf_op jit(solution)/shard_map/reduce_scatter | solution.py:222
  411.3 431.6 %reduce-scatter.18.cloned.1.call-start = ((), (), s32[]{:S(2)}) async-start(), calls=%async_computation.18 | async-start | bytes 5013504 | tf_op jit(solution)/shard_map/reduce_scatter | solution.py:226
  416.4 1.3 copy-start.22
  416.5 506.0 %reduce-scatter.20.cloned.1.call-start = ((), (), s32[]{:S(2)}) async-start(), calls=%async_computation.19 | async-start | bytes 5013504 | tf_op jit(solution)/shard_map/reduce_scatter | solution.py:227
  422.9 571.1 %reduce-scatter.10.cloned.1.call-start = ((), (), s32[]{:S(2)}) async-start(), calls=%async_computation.14 | async-start | bytes 3760128 | tf_op jit(solution)/shard_map/reduce_scatter | solution.py:221
  427.0 92.8 %copy-start.51 = (f32[448]{0:T(512)S(1)}, f32[448]{0:T(512)}, u32[]{:S(2)}) copy-start(f32[448]{0:T(512)} %copy-done.50) | copy-start | bytes 5380
  518.0 1.9 copy-start.15
  582.6 411.3 %copy-start.1 = (bf16[768,1536]{1,0:T(8,128)(2,1)S(1)}, bf16[768,1536]{1,0:T(8,128)(2,1)}, u32[]{:S(2)}) copy-start(bf16[768,1536]{1,0:T(8,128)(2,1)} %param.28) | copy-start | bytes 7077892
  (21 other events, 20.6 us)
Sparse Core Ops, SparseCore 0:
  31.7 49.8 all-reduce.9
  117.3 47.1 all-reduce.11
  179.3 47.1 all-reduce.13
  238.2 47.1 all-reduce.15
  318.9 47.1 all-reduce.17
  370.0 99.2 all-reduce.21
  471.7 46.2 all-reduce.19
  520.3 58.9 reduce-scatter.7
  583.4 58.0 reduce-scatter.15
  645.6 57.0 reduce-scatter.13
  706.9 57.1 reduce-scatter.11
  768.3 74.5 reduce-scatter.17
  847.8 74.5 reduce-scatter.19
  926.8 67.1 reduce-scatter.9
where the time goes:
time: 1010 us; the launch traced here: 1000 us
  waiting for transfers between devices  690 us (68%)
  matrix products  126 us (12%)
  blocking collectives  62 us (6%)
  local copies, waits for them, and re-layouts  55.9 us (6%)
  other arithmetic  48.1 us (5%)
  between operations  16.6 us (2%)
    reduce_scatter x1, waiting for transfers between devices, on_device(): lax.psum_scatter(second_dense_gradient, 'dp', scatter_dimension=1, tiled=...  79.5 us
    reduce_scatter x1, waiting for transfers between devices, on_device(): lax.psum_scatter(fc1_grad, 'dp', scatter_dimension=0, tiled=True)  78.9 us
    reduce_scatter x1, waiting for transfers between devices, on_device(): lax.psum_scatter(self_qkv_grad, 'dp', scatter_dimension=0, tiled=True)  71.5 us
    psum x1, blocking collectives, on_device(): lax.psum((self_qv_bias_grad, cross_bias_grad, fc1_bias_grad, out_biases_g...  62 us
    reduce_scatter x1, waiting for transfers between devices, on_device(): lax.psum_scatter(self_out_grad, 'dp', scatter_dimension=1, tiled=True)  61.3 us
    reduce_scatter x1, waiting for transfers between devices, on_device(): lax.psum_scatter(cross_q_grad, 'dp', scatter_dimension=0, tiled=True)  61.1 us
    reduce_scatter x1, waiting for transfers between devices, on_device(): lax.psum_scatter(cross_out_grad, 'dp', scatter_dimension=1, tiled=True)  49.1 us
    psum x1, waiting for transfers between devices, on_device(): stream_three = stream_two + lax.psum(dense_portion, 'mp') + out_biases[2]  47.3 us
  transfers between devices with their start and end apart: 14, of which 13 were waited for; matrix products, arithmetic and copies ran while one was open for 10% of the time, Pallas kernels for 0%

commit v1 on v0

v1 whole, which is shorter than its diff:
```python
from functools import partial

import jax
import jax.numpy as jnp
from jax import lax
from jax.sharding import PartitionSpec as P

HEAD_DIM = 64


def norm_rows(stream, norm_gain, norm_shift):
    centred = stream - jnp.mean(stream, axis=-1, keepdims=True)
    spread = jnp.mean(centred * centred, axis=-1, keepdims=True)
    return centred * lax.rsqrt(spread + 1e-05) * norm_gain + norm_shift


def split_heads(flat_rows):
    return flat_rows.reshape(flat_rows.shape[0], -1, HEAD_DIM)


def join_heads(headed):
    return headed.reshape(headed.shape[0], -1)


def dot(a, b):
    return lax.dot_general(a, b, (((1,), (0,)), ((), ())), preferred_element_type=jnp.float32)


def dot_nt(a, b):
    return lax.dot_general(a, b, (((1,), (1,)), ((), ())), preferred_element_type=jnp.float32)


def dot_tn(a, b):
    return lax.dot_general(a, b, (((0,), (0,)), ((), ())), preferred_element_type=jnp.float32)


def score_block(query_rows, key_rows, key_mask):
    scores = jnp.einsum("qhd,khd->hqk", query_rows, key_rows, preferred_element_type=jnp.float32)
    if key_mask is not None:
        scores = jnp.where(key_mask, scores, -1e30)
    return scores


def attend_forward(query_rows, key_rows, value_rows, key_mask):
    scores = score_block(query_rows, key_rows, key_mask)
    highest = jnp.max(scores, axis=-1, keepdims=True)
    log_total = highest + jnp.log(jnp.sum(jnp.exp(scores - highest), axis=-1, keepdims=True))
    weights = jnp.exp(scores - log_total).astype(jnp.bfloat16)
    mixed_heads = jnp.einsum("hqk,khd->qhd", weights, value_rows, preferred_element_type=jnp.float32)
    return (join_heads(mixed_heads).astype(jnp.bfloat16), log_total)


def attend_backward(query_rows, key_rows, value_rows, key_mask, log_total, grad_mixed):
    grad_heads = split_heads(grad_mixed)
    softmax_out = jnp.exp(score_block(query_rows, key_rows, key_mask) - log_total)
    weights = softmax_out.astype(jnp.bfloat16)
    grad_probs = jnp.einsum("qhd,khd->hqk", grad_heads, value_rows, preferred_element_type=jnp.float32)
    inner_sum = jnp.sum(softmax_out * grad_probs, axis=-1, keepdims=True)
    grad_scores = (softmax_out * (grad_probs - inner_sum)).astype(jnp.bfloat16)
    grad_queries = jnp.einsum("hqk,khd->qhd", grad_scores, key_rows, preferred_element_type=jnp.float32)
    grad_keys = jnp.einsum("hqk,qhd->khd", grad_scores, query_rows, preferred_element_type=jnp.float32)
    grad_values = jnp.einsum("hqk,qhd->khd", weights, grad_heads, preferred_element_type=jnp.float32)
    return (
        join_heads(grad_queries).astype(jnp.bfloat16),
        join_heads(grad_keys).astype(jnp.bfloat16),
        join_heads(grad_values).astype(jnp.bfloat16),
    )


def row_total(matrix_rows):
    return jnp.sum(matrix_rows, axis=0, dtype=jnp.float32)


def swap_mp(v):
    return lax.ppermute(v, "mp", [(0, 1), (1, 0)])


def swap_dp(v, bit, dp_size):
    return lax.ppermute(v, "dp", [(i, i ^ bit) for i in range(dp_size)])


def relative_order(width, dp_size):
    shard = width // dp_size
    bits = dp_size.bit_length() - 1
    me = lax.axis_index("dp")
    place = jnp.arange(width, dtype=jnp.int32)
    block = place // shard
    flipped = jnp.zeros_like(block)
    for step in range(bits):
        flipped = flipped + (((block >> step) & 1) << (bits - 1 - step))
    source = (flipped ^ me) * shard + place % shard
    rows = jnp.arange(width, dtype=jnp.int32)
    return (rows[:, None] == source[None, :]).astype(jnp.bfloat16)


def halving(lhs, rhs, dp_size):
    width = lhs.shape[1]
    half = width // 2
    sent = swap_dp(dot_tn(lhs[:, half:], rhs), 1, dp_size)
    kept = dot_tn(lhs[:, :half], rhs) + sent
    bit = 2
    while bit < dp_size:
        half = kept.shape[0] // 2
        kept = kept[:half] + swap_dp(kept[half:], bit, dp_size)
        bit *= 2
    return kept


def on_device(
    dp_size,
    tokens,
    frames,
    lengths,
    out_cot,
    self_query_key_value,
    self_qv_bias,
    self_output_weight,
    cross_query_weight,
    cross_kv,
    cross_bias,
    cross_output_weight,
    first_dense_weight,
    first_dense_bias,
    second_dense_weight,
    out_biases,
    norm_gains,
    norm_biases,
):
    _, slot_len, model_width = tokens.shape
    tokens, frames, out_cot = tokens[0], frames[0], out_cot[0]
    own = self_output_weight.shape[0]
    order = relative_order(model_width, dp_size)

    def reorder(lhs):
        return dot(lhs, order).astype(jnp.bfloat16)

    positions = jnp.arange(slot_len, dtype=jnp.int32)
    valid = (positions < lengths[0]).astype(jnp.float32)[:, None]
    causal = positions[None, :] <= positions[:, None]
    key_mask = (causal & (positions[None, :] < lengths[0]))[None]
    qkv_weight = self_query_key_value.reshape(model_width, -1)
    kv_weight = cross_kv.reshape(model_width, -1)
    stream_zero = tokens.astype(jnp.float32)
    normed_one, pull_one = jax.vjp(norm_rows, stream_zero, norm_gains[0], norm_biases[0])
    first_input = normed_one.astype(jnp.bfloat16)
    merged = dot(first_input, qkv_weight)
    queries_self = split_heads(((merged[:, :own] + self_qv_bias[0]) * 0.125).astype(jnp.bfloat16))
    keys_self = split_heads(merged[:, own : 2 * own].astype(jnp.bfloat16))
    values_self = split_heads((merged[:, 2 * own :] + self_qv_bias[1]).astype(jnp.bfloat16))
    self_mixture, lse_self = attend_forward(queries_self, keys_self, values_self, key_mask)
    self_portion = dot(self_mixture, self_output_weight)
    stream_one = stream_zero + (self_portion + swap_mp(self_portion)) + out_biases[0]
    normed_two, pull_two = jax.vjp(norm_rows, stream_one, norm_gains[1], norm_biases[1])
    second_input = normed_two.astype(jnp.bfloat16)
    query_projected = dot(second_input, cross_query_weight)
    queries_cross = split_heads(((query_projected + cross_bias[0]) * 0.125).astype(jnp.bfloat16))
    frame_pair = dot(frames, kv_weight)
    keys_cross = split_heads(frame_pair[:, :own].astype(jnp.bfloat16))
    values_cross = split_heads((frame_pair[:, own:] + cross_bias[1]).astype(jnp.bfloat16))
    cross_mixture, lse_cross = attend_forward(queries_cross, keys_cross, values_cross, None)
    part_cross = dot(cross_mixture, cross_output_weight)
    stream_two = stream_one + (part_cross + swap_mp(part_cross)) + out_biases[1]
    normed_three, pull_three = jax.vjp(norm_rows, stream_two, norm_gains[2], norm_biases[2])
    third_input = normed_three.astype(jnp.bfloat16)
    hidden = dot(third_input, first_dense_weight) + first_dense_bias
    active, gelu_pull = jax.vjp(partial(jax.nn.gelu, approximate=False), hidden)
    active_reduced = active.astype(jnp.bfloat16)
    dense_portion = dot(active_reduced, second_dense_weight)
    stream_three = stream_two + (dense_portion + swap_mp(dense_portion)) + out_biases[2]
    final_norm, pull_four = jax.vjp(norm_rows, stream_three, norm_gains[3], norm_biases[3])
    output = (final_norm * valid).astype(jnp.bfloat16)
    grad_three, gain_four, shift_four = pull_four(out_cot.astype(jnp.float32) * valid)
    reduced_third = grad_three.astype(jnp.bfloat16)
    active_gradient = dot_nt(reduced_third, second_dense_weight)
    reduced_hidden = gelu_pull(active_gradient)[0].astype(jnp.bfloat16)
    reverse_third = dot_nt(reduced_hidden, first_dense_weight)
    swapped_third = swap_mp(reverse_third)
    second_dense_gradient = halving(reorder(reduced_third), active_reduced, dp_size)
    fc1_grad = halving(reorder(third_input), reduced_hidden, dp_size)
    fc1_bias_grad = row_total(reduced_hidden)
    grad_part_two, gain_three, shift_three = pull_three(reverse_third + swapped_third)
    grad_two = grad_three + grad_part_two
    reduced_second = grad_two.astype(jnp.bfloat16)
    cross_out_grad = halving(reorder(reduced_second), cross_mixture, dp_size)
    grad_mixed_cross = dot_nt(reduced_second, cross_output_weight).astype(jnp.bfloat16)
    grad_qc, grad_kc, grad_vc = attend_backward(
        queries_cross, keys_cross, values_cross, None, lse_cross, grad_mixed_cross
    )
    reduced_cross_query = grad_qc * 0.125
    back_two = dot_nt(reduced_cross_query, cross_query_weight)
    swapped_two = swap_mp(back_two)
    low_frame_pair = jnp.concatenate([grad_kc, grad_vc], axis=1)
    cross_q_grad = halving(reorder(second_input), reduced_cross_query, dp_size)
    cross_kv_grad = halving(reorder(frames), low_frame_pair, dp_size)
    my_part = lax.axis_index("mp")
    frame_width = model_width // 2
    other_weight = lax.dynamic_slice_in_dim(kv_weight, (1 - my_part) * frame_width, frame_width, 0)
    own_weight = lax.dynamic_slice_in_dim(kv_weight, my_part * frame_width, frame_width, 0)
    sent_frames = swap_mp(dot_nt(low_frame_pair, other_weight))
    frames_grad = dot_nt(low_frame_pair, own_weight) + sent_frames
    grad_part_one, gain_two, shift_two = pull_two(back_two + swapped_two)
    grad_one = grad_two + grad_part_one
    reduced_first = grad_one.astype(jnp.bfloat16)
    self_out_grad = halving(reorder(reduced_first), self_mixture, dp_size)
    grad_mixed_self = dot_nt(reduced_first, self_output_weight).astype(jnp.bfloat16)
    grad_qs, grad_ks, grad_vs = attend_backward(
        queries_self, keys_self, values_self, key_mask, lse_self, grad_mixed_self
    )
    low_query_self = grad_qs * 0.125
    reduced_merged = jnp.concatenate([low_query_self, grad_ks, grad_vs], axis=1)
    reverse_first = dot_nt(reduced_merged, qkv_weight)
    swapped_first = swap_mp(reverse_first)
    self_qkv_grad = halving(reorder(first_input), reduced_merged, dp_size)
    grad_part_zero, gain_one, shift_one = pull_one(reverse_first + swapped_first)
    tokens_grad = grad_one + grad_part_zero
    small = [
        row_total(low_query_self),
        row_total(grad_vs),
        row_total(reduced_cross_query),
        row_total(grad_vc),
        fc1_bias_grad,
        row_total(grad_one),
        row_total(grad_two),
        row_total(grad_three),
        gain_one,
        gain_two,
        gain_three,
        gain_four,
        shift_one,
        shift_two,
        shift_three,
        shift_four,
    ]
    total = jnp.concatenate(small)
    bit = 1
    while bit < dp_size:
        total = total + swap_dp(total, bit, dp_size)
        bit *= 2
    pieces = []
    at = 0
    for item in small:
        pieces.append(total[at : at + item.shape[0]])
        at += item.shape[0]
    shard = model_width // dp_size
    return (
        output[None],
        tokens_grad[None],
        frames_grad[None],
        self_qkv_grad.reshape(shard, 3, own),
        jnp.stack(pieces[0:2]),
        self_out_grad.T,
        cross_q_grad,
        cross_kv_grad.reshape(shard, 2, own),
        jnp.stack(pieces[2:4]),
        cross_out_grad.T,
        fc1_grad,
        pieces[4],
        second_dense_gradient.T,
        jnp.stack(pieces[5:8]),
        jnp.stack(pieces[8:12]),
        jnp.stack(pieces[12:16]),
    )


def solution(mesh):
    in_specs = (
        P("dp", None, None),
        P("dp", None, None),
        P("dp"),
        P("dp", None, None),
        P(None, None, "mp"),
        P(None, "mp"),
        P("mp", None),
        P(None, "mp"),
        P(None, None, "mp"),
        P(None, "mp"),
        P("mp", None),
        P(None, "mp"),
        P("mp"),
        P("mp", None),
        P(),
        P(),
        P(),
    )
    out_specs = (
        P("dp", None, None),
        P("dp", None, None),
        P("dp", None, "mp"),
        P("dp", None, "mp"),
        P(None, "mp"),
        P("mp", "dp"),
        P("dp", "mp"),
        P("dp", None, "mp"),
        P(None, "mp"),
        P("mp", "dp"),
        P("dp", "mp"),
        P("mp"),
        P("mp", "dp"),
        P(),
        P(),
        P(),
    )
    return jax.shard_map(
        partial(on_device, mesh.shape["dp"]),
        mesh=mesh,
        in_specs=in_specs,
        out_specs=out_specs,
        check_vma=False,
    )
```

time: 1010 us -> 493 us (0.49)
  waiting for transfers between devices: 690 us -> 200 us
  blocking collectives: 62 us -> 0 us
  starting transfers between devices: 1.84 us -> 41.5 us
  between operations: 16.6 us -> 3.76 us
  other arithmetic: 48.1 us -> 60.4 us
    reduce_scatter x7 -> x0, waiting for transfers between devices: 401 us -> none  [the longest x1 79.5 us: on_device(): lax.psum_scatter(second_dense_gradient, 'dp', scatter_dimension=1, tiled=...]
    psum x6 -> x0, waiting for transfers between devices: 249 us -> none  [the longest x1 47.3 us: on_device(): stream_three = stream_two + lax.psum(dense_portion, 'mp') + out_biases[2]]
    ppermute x0 -> x39, waiting for transfers between devices: none -> 200 us  [the longest x32 112 us: swap_dp(): return lax.ppermute(v, 'dp', [(i, i ^ bit) for i in range(dp_size)])]
    psum x1 -> x0, blocking collectives: 62 us -> none  [on_device(): lax.psum((self_qv_bias_grad, cross_bias_grad, fc1_bias_grad, out_biases_g...]
    ppermute x0 -> x39, starting transfers between devices: none -> 41.5 us  [the longest x32 31.9 us: swap_dp(): return lax.ppermute(v, 'dp', [(i, i ^ bit) for i in range(dp_size)])]
    unnamed x15 -> x0, waiting for transfers between devices: 40.4 us -> none
    dot_general x33 -> x48, matrix products: 126 us -> 130 us  [the longest x14 31.1 us: dot(): lax.dot_general(a, b, (((1,), (0,)), ((), ())), preferred_element_type=jn...]
    unnamed x145 -> x238, local copies, waits for them, and re-layouts: 27.3 us -> 24.1 us
  transfers between devices with their start and end apart: 14 -> 39, of which waited for: 13 -> 20; matrix products, arithmetic and copies ran while one was open for 10% -> 31% of each run, Pallas kernels for 0% -> 0%
where the time goes in v1:
time: 493 us; the launch traced here: 485 us
  waiting for transfers between devices  200 us (41%)
  matrix products  130 us (26%)
  other arithmetic  60.4 us (12%)
  local copies, waits for them, and re-layouts  49.6 us (10%)
  starting transfers between devices  41.5 us (8%)
    ppermute x32, waiting for transfers between devices, swap_dp(): return lax.ppermute(v, 'dp', [(i, i ^ bit) for i in range(dp_size)])  112 us
    ppermute x7, waiting for transfers between devices, swap_mp(): return lax.ppermute(v, 'mp', [(0, 1), (1, 0)])  88 us
    ppermute x32, starting transfers between devices, swap_dp(): return lax.ppermute(v, 'dp', [(i, i ^ bit) for i in range(dp_size)])  31.9 us
    dot_general x14, matrix products, dot(): lax.dot_general(a, b, (((1,), (0,)), ((), ())), preferred_element_type=jn...  31.1 us
    dot_general x14, matrix products, dot_tn(): lax.dot_general(a, b, (((0,), (0,)), ((), ())), preferred_element_type=jn...  24.3 us
    unnamed x238, local copies, waits for them, and re-layouts  24.1 us
    dot_general x8, matrix products, dot_nt(): lax.dot_general(a, b, (((1,), (1,)), ((), ())), preferred_element_type=jn...  17.7 us
    dot_general x2, matrix products, attend_backward(): jnp.einsum('qhd,khd->hqk', grad_heads, value_rows, preferred_element_type...  15.8 us
  transfers between devices with their start and end apart: 39, of which 20 were waited for; matrix products, arithmetic and copies ran while one was open for 31% of the time, Pallas kernels for 0%

profile of v1, /device:TPU:0, one launch (start us, length us, event | category | flops | bytes accessed | tf_op | source)
XLA Modules:
  0.0 484.8 jit_solution(2437532948449377082)
XLA Ops:
  5.0 3.9 copy.55
  9.6 2.7 fusion.74
  15.9 1.9 copy.58
  17.8 1.9 copy.56
  19.7 2.1 select_reduce_fusion
  27.3 2.9 collective-permute-start
  30.6 2.0 fusion.18
  32.6 2.1 copy-done.36
  35.8 2.4 copy.62
  38.2 2.8 fusion.16
  41.0 2.6 copy.60
  44.2 16.6 %collective-permute-done = f32[448,768]{1,0:T(8,128)} collective-permute-done((f32[448,768]{1,0:T(8,128)}, f32[448,768]{1,0:T(8,128)}, u32[]{:S(2)}, u32[]{:S(2)}) %collective-permute-start) | collective-permute-done | bytes 1376288 | tf_op jit(solution)/shard_map/ppermute | solution.py:75
  60.8 2.1 fusion.147
  67.2 9.4 %fusion.151 = (f32[6,448]{1,0:T(8,128)S(1)}, f32[6,448,1500]{2,1,0:T(8,128)}) fusion(bf16[448,6,64]{0,2,1:T(8,128)(2,1)S(1)} %bitcast.171, bf16[1500,6,64]{0,2,1:T(8,128)(2,1)} %bitcast.161), kind=kOutput, calls=%fused_computation.301 | convolution fusion | flops 520125312 | bytes 17634816 | tf_op jit(solution)/shard_map/qhd,khd->hqk/dot_general | solution.py:38
  76.6 8.2 %exponential_reduce_fusion = f32[6,448]{1,0:T(8,128)S(1)} fusion(f32[6,448,1500]{2,1,0:T(8,128)} %get-tuple-element.119, f32[6,448]{1,0:T(8,128)S(1)} %get-tuple-element.118), kind=kLoop, calls=%fused_computation.3 | loop fusion | flops 8061312 | bytes 16149504 | tf_op jit(solution)/shard_map/reduce_sum | solution.py:47
  84.8 8.3 %fusion.55 = bf16[6,64,448]{2,1,0:T(8,128)(2,1)S(1)} fusion(bf16[1500,6,64]{0,2,1:T(8,128)(2,1)S(1)} %bitcast.163, f32[6,448,1500]{2,1,0:T(8,128)} %get-tuple-element.119, f32[6,448]{1,0:T(8,128)S(1)} %log_add_fusion), kind=kOutput, calls=%fused_computation.112 | convolution fusion | flops 524332032 | bytes 17634816 | tf_op jit(solution)/shard_map/hqk,khd->qhd/dot_general | solution.py:49
  95.5 29.6 %collective-permute-done.1 = f32[448,768]{1,0:T(8,128)S(1)} collective-permute-done((f32[448,768]{1,0:T(8,128)S(1)}, f32[448,768]{1,0:T(8,128)S(1)}, u32[]{:S(2)}, u32[]{:S(2)}) %collective-permute-start.1) | collective-permute-done | bytes 1376288 | tf_op jit(solution)/shard_map/ppermute | solution.py:75
  126.1 8.6 %multiply_convert_fusion.2 = (bf16[448,1536]{1,0:T(8,128)(2,1)S(1)}, f32[448,1536]{1,0:T(8,128)}, f32[448,1536]{1,0:T(8,128)}) fusion(f32[1536]{0:T(1024)S(1)} %copy-done.103, bf16[768,1536]{1,0:T(8,128)(2,1)S(1)} %copy-done, f32[448,768]{1,0:T(8,128)S(1)} %get-tuple-element.94, f32[768]{0:T(1024)S(1)} %get-tuple-element.68, ...), kind=kOutput, calls=%fused_computation.25 | convolution fusion | flops 1104101376 | bytes 10632704 | tf_op jit(solution)/shard_map/dot_general | solution.py:26
  134.7 2.3 fusion.154
  138.5 2.7 fusion.48
  141.2 3.4 fusion.3
  144.7 23.1 %collective-permute-done.2 = f32[448,768]{1,0:T(8,128)} collective-permute-done((f32[448,768]{1,0:T(8,128)}, f32[448,768]{1,0:T(8,128)}, u32[]{:S(2)}, u32[]{:S(2)}) %collective-permute-start.2) | collective-permute-done | bytes 1376288 | tf_op jit(solution)/shard_map/ppermute | solution.py:75
  167.8 2.2 fusion.144
  174.1 2.7 convert_reduce_fusion
  182.8 2.2 fusion.94
  186.3 2.2 fusion.91
  189.0 18.7 %collective-permute-done.3 = f32[448,768]{1,0:T(8,128)S(1)} collective-permute-done((f32[448,768]{1,0:T(8,128)S(1)}, f32[448,768]{1,0:T(8,128)S(1)}, u32[]{:S(2)}, u32[]{:S(2)}) %collective-permute-start.3) | collective-permute-done | bytes 1376288 | tf_op jit(solution)/shard_map/ppermute | solution.py:75
  211.3 9.2 %convert_reduce_fusion.1 = (f32[6,64]{1,0:T(8,128)}, bf16[6,64,1500]{2,1,0:T(8,128)(2,1)S(1)}) fusion(bf16[448,6,64]{0,2,1:T(8,128)(2,1)S(1)} %bitcast.173, f32[6,448,1500]{2,1,0:T(8,128)} %get-tuple-element.119, f32[6,448]{1,0:T(8,128)S(1)} %log_add_fusion), kind=kOutput, calls=%fused_computation.40 | convolution fusion | flops 525887616 | bytes 17636352 | tf_op jit(solution)/shard_map/hqk,qhd->khd/dot_general | solution.py:62
  220.5 11.2 %multiply_reduce_fusion = (f32[6,448]{1,0:T(8,128)S(1)}, f32[6,448,1500]{2,1,0:T(8,128)}) fusion(f32[6,448,1500]{2,1,0:T(8,128)} %get-tuple-element.119, f32[6,448]{1,0:T(8,128)S(1)} %log_add_fusion, bf16[448,6,64]{0,2,1:T(8,128)(2,1)S(1)} %bitcast.174, bf16[1500,6,64]{0,2,1:T(8,128)(2,1)S(1)} %bitcast.164), kind=kOutput, calls=%fused_computation.1 | convolution fusion | flops 528189312 | bytes 33773568 | tf_op jit(solution)/shard_map/qhd,khd->hqk/dot_general | solution.py:57
  231.7 11.9 %multiply_convert_fusion = bf16[6,448,1500]{2,1,0:T(8,128)(2,1)S(1)} fusion(f32[6,448,1500]{2,1,0:T(8,128)} %get-tuple-element.122, f32[6,448,1500]{2,1,0:T(8,128)} %get-tuple-element.119, f32[6,448]{1,0:T(8,128)S(1)} %get-tuple-element.121, f32[6,448]{1,0:T(8,128)S(1)} %log_add_fusion), kind=kLoop, calls=%fused_computation | loop fusion | flops 16128000 | bytes 40341504 | tf_op jit(solution)/shard_map/convert_element_type | solution.py:59
  243.6 2.5 convert_reduce_fusion.3
  250.4 2.2 fusion.68
  258.5 2.9 fusion.88
  262.7 3.3 collective-permute-done.28
  266.9 4.5 collective-permute-done.20
  274.0 3.0 convolution_add_fusion.4
  277.6 2.7 convolution_add_fusion.3
  284.2 2.7 collective-permute-start.30
  286.9 2.6 collective-permute-done.30
  289.5 2.7 collective-permute-start.22
  296.0 2.5 convolution_add_fusion.5
  301.0 2.6 multiply_reduce_fusion.3
  308.4 4.8 convert_reduce_fusion.4
  313.2 4.6 multiply_reduce_fusion.1
  321.6 2.2 fusion.103
  323.9 3.9 fusion.136
  327.9 1.9 fusion.106
  329.8 17.6 %collective-permute-done.24 = f32[192,768]{1,0:T(8,128)} collective-permute-done((f32[192,768]{1,0:T(8,128)}, f32[192,768]{1,0:T(8,128)}, u32[]{:S(2)}, u32[]{:S(2)}) %collective-permute-start.24) | collective-permute-done | bytes 589856 | tf_op jit(solution)/shard_map/ppermute | solution.py:79
  351.9 3.5 collective-permute-done.25
  358.5 2.7 collective-permute-start.26
  366.7 2.0 collective-permute-done.26
  369.6 14.8 %collective-permute-done.17 = f32[96,384]{1,0:T(8,128)S(1)} collective-permute-done((f32[96,384]{1,0:T(8,128)}, f32[96,384]{1,0:T(8,128)S(1)}, u32[]{:S(2)}, u32[]{:S(2)}) %collective-permute-start.17) | collective-permute-done | bytes 147488 | tf_op jit(solution)/shard_map/ppermute | solution.py:79
  384.4 3.7 collective-permute-start.18
  388.1 4.3 fusion.2
  392.4 8.0 %copy.68 = f32[1,1500,384]{2,0,1:T(1,128)} copy(f32[1,1500,384]{2,1,0:T(8,128)S(1)} %fusion.2) | data formatting | bytes 4608000
  401.1 2.2 fusion.138
  407.9 1.9 collective-permute-done.12
  409.8 2.9 collective-permute-start.13
  414.8 2.2 collective-permute-start.14
  418.0 19.2 %collective-permute-done.14 = f32[11520]{0:T(1024)S(1)} collective-permute-done((f32[11520]{0:T(1024)S(1)}, f32[11520]{0:T(1024)S(1)}, u32[]{:S(2)}, u32[]{:S(2)}) %collective-permute-start.14) | collective-permute-done | bytes 46112 | tf_op jit(solution)/shard_map/ppermute | solution.py:79
  437.2 2.2 convolution_add_fusion
  443.8 17.2 %collective-permute-done.8 = f32[192,1152]{1,0:T(8,128)S(1)} collective-permute-done((f32[192,1152]{1,0:T(8,128)S(1)}, f32[192,1152]{1,0:T(8,128)S(1)}, u32[]{:S(2)}, u32[]{:S(2)}) %collective-permute-start.8) | collective-permute-done | bytes 884768 | tf_op jit(solution)/shard_map/ppermute | solution.py:79
  462.0 10.4 %collective-permute-done.9 = f32[96,1152]{1,0:T(8,128)S(1)} collective-permute-done((f32[96,1152]{1,0:T(8,128)S(1)}, f32[96,1152]{1,0:T(8,128)S(1)}, u32[]{:S(2)}, u32[]{:S(2)}) %collective-permute-start.9) | collective-permute-done | bytes 442400 | tf_op jit(solution)/shard_map/ppermute | solution.py:79
  473.3 10.3 %collective-permute-done.10 = f32[48,1152]{1,0:T(8,128)S(1)} collective-permute-done((f32[48,1152]{1,0:T(8,128)S(1)}, f32[48,1152]{1,0:T(8,128)S(1)}, u32[]{:S(2)}, u32[]{:S(2)}) %collective-permute-start.10) | collective-permute-done | bytes 221216 | tf_op jit(solution)/shard_map/ppermute | solution.py:79
  (440 shorter events, 102.4 us)
Async XLA Ops:
  0.6 125.1 %copy-start = (bf16[768,1536]{1,0:T(8,128)(2,1)S(1)}, bf16[768,1536]{1,0:T(8,128)(2,1)}, u32[]{:S(2)}) copy-start(bf16[768,1536]{1,0:T(8,128)(2,1)} %param.28) | copy-start | bytes 7077892
  4.9 18.0 %copy-start.21 = (pred[448,448]{0,1:T(8,128)(4,1)}, pred[448,448]{0,1:T(8,128)(4,1)S(1)}, u32[]{:S(2)}) copy-start(pred[448,448]{0,1:T(8,128)(4,1)S(1)} %fusion.71) | copy-start | bytes 602116
  9.6 116.2 %copy-start.92 = (f32[768]{0:T(1024)}, f32[768]{0:T(1024)S(1)}, u32[]{:S(2)}) copy-start(f32[768]{0:T(1024)S(1)} %get-tuple-element.68) | copy-start | bytes 9220
  27.3 33.4 %collective-permute-start = (f32[448,768]{1,0:T(8,128)}, f32[448,768]{1,0:T(8,128)}, u32[]{:S(2)}, u32[]{:S(2)}) collective-permute-start(f32[448,768]{1,0:T(8,128)} %fusion.152), channel_id=1, source_target_pairs={{0,1},{1,0},{2,3},{3,2},{4,5},{5,4},{6,7},{7,6},{8,9},{9,8},{10,11... | collective-permute-start | bytes 4128776 | tf_op jit(solution)/shard_map/ppermute | solution.py:75
  67.2 9.4 %copy-start.19 = (bf16[448,384]{0,1:T(8,128)(2,1)}, bf16[448,384]{0,1:T(8,128)(2,1)S(1)}, u32[]{:S(2)}) copy-start(bf16[448,384]{0,1:T(8,128)(2,1)S(1)} %copy.61) | copy-start | bytes 1032196
  93.1 32.0 %copy-start.4 = (f32[448,768]{1,0:T(8,128)S(1)}, f32[448,768]{1,0:T(8,128)}, u32[]{:S(2)}) copy-start(f32[448,768]{1,0:T(8,128)} %copy-done.3) | copy-start | bytes 4128772
  93.7 31.4 %collective-permute-start.1 = (f32[448,768]{1,0:T(8,128)S(1)}, f32[448,768]{1,0:T(8,128)S(1)}, u32[]{:S(2)}, u32[]{:S(2)}) collective-permute-start(f32[448,768]{1,0:T(8,128)S(1)} %fusion.153), channel_id=1, source_target_pairs={{0,1},{1,0},{2,3},{3,2},{4,5},{5,4},{6,7},{7,6},{8,9},{9,8},{10,11... | collective-permute-start | bytes 4128776 | tf_op jit(solution)/shard_map/ppermute | solution.py:75
  125.4 9.3 %copy-start.6 = (f32[448,768]{1,0:T(8,128)}, f32[448,768]{1,0:T(8,128)S(1)}, u32[]{:S(2)}) copy-start(f32[448,768]{1,0:T(8,128)S(1)} %get-tuple-element.94) | copy-start | bytes 4128772
  137.0 30.8 %collective-permute-start.2 = (f32[448,768]{1,0:T(8,128)}, f32[448,768]{1,0:T(8,128)}, u32[]{:S(2)}, u32[]{:S(2)}) collective-permute-start(f32[448,768]{1,0:T(8,128)} %fusion.154), channel_id=1, source_target_pairs={{0,1},{1,0},{2,3},{3,2},{4,5},{5,4},{6,7},{7,6},{8,9},{9,8},{10,11... | collective-permute-start | bytes 4128776 | tf_op jit(solution)/shard_map/ppermute | solution.py:75
  138.5 46.5 %copy-start.95 = (s32[768]{0:T(1024)}, s32[768]{0:T(1024)S(1)}, u32[]{:S(2)}) copy-start(s32[768]{0:T(1024)S(1)} %fusion.124) | copy-start | bytes 9220
  141.2 26.6 %copy-start.7 = (f32[448,768]{1,0:T(8,128)S(1)}, f32[448,768]{1,0:T(8,128)}, u32[]{:S(2)}) copy-start(f32[448,768]{1,0:T(8,128)} %copy-done.6) | copy-start | bytes 4128772
  141.2 26.6 %copy-start.84 = (f32[768]{0:T(1024)S(1)}, f32[768]{0:T(1024)}, u32[]{:S(2)}) copy-start(f32[768]{0:T(1024)} %get-tuple-element.69) | copy-start | bytes 9220
  178.1 29.6 %collective-permute-start.3 = (f32[448,768]{1,0:T(8,128)S(1)}, f32[448,768]{1,0:T(8,128)S(1)}, u32[]{:S(2)}, u32[]{:S(2)}) collective-permute-start(f32[448,768]{1,0:T(8,128)S(1)} %fusion.155), channel_id=1, source_target_pairs={{0,1},{1,0},{2,3},{3,2},{4,5},{5,4},{6,7},{7,6},{8,9},{9,8},{10,11... | collective-permute-start | bytes 4128776 | tf_op jit(solution)/shard_map/ppermute | solution.py:75
  185.0 87.3 %collective-permute-start.31 = (f32[384,1536]{1,0:T(8,128)}, f32[384,1536]{1,0:T(8,128)}, u32[]{:S(2)}, u32[]{:S(2)}) collective-permute-start(f32[384,1536]{1,0:T(8,128)} %fusion.94), channel_id=1, source_target_pairs={{0,2},{2,0},{4,6},{6,4},{8,10},{10,8},{12,14},{14,12},{16,18},{18,... | collective-permute-start | bytes 7077896 | tf_op jit(solution)/shard_map/ppermute | solution.py:79
  188.5 20.3 %copy-start.74 = (f32[448]{0:T(512)S(1)}, f32[448]{0:T(512)}, u32[]{:S(2)}) copy-start(f32[448]{0:T(512)} %copy-done.73) | copy-start | bytes 5380
  188.5 88.4 %collective-permute-start.35 = (f32[384,1536]{1,0:T(8,128)}, f32[384,1536]{1,0:T(8,128)}, u32[]{:S(2)}, u32[]{:S(2)}) collective-permute-start(f32[384,1536]{1,0:T(8,128)} %fusion.91), channel_id=1, source_target_pairs={{0,2},{2,0},{4,6},{6,4},{8,10},{10,8},{12,14},{14,12},{16,18},{18,... | collective-permute-start | bytes 7077896 | tf_op jit(solution)/shard_map/ppermute | solution.py:79
  211.3 9.2 %copy-start.14 = (bf16[1500,384]{0,1:T(8,128)(2,1)S(1)}, bf16[1500,384]{0,1:T(8,128)(2,1)}, u32[]{:S(2)}) copy-start(bf16[1500,384]{0,1:T(8,128)(2,1)} %copy.60) | copy-start | bytes 3456004
  220.5 38.0 %copy-start.47 = (bf16[6,64,1500]{2,1,0:T(8,128)(2,1)}, bf16[6,64,1500]{2,1,0:T(8,128)(2,1)S(1)}, u32[]{:S(2)}) copy-start(bf16[6,64,1500]{2,1,0:T(8,128)(2,1)S(1)} %get-tuple-element.132) | copy-start | bytes 3456004
  231.7 11.9 %copy-start.9 = (bf16[1500,384]{0,1:T(8,128)(2,1)S(1)}, bf16[1500,384]{0,1:T(8,128)(2,1)}, u32[]{:S(2)}) copy-start(bf16[1500,384]{0,1:T(8,128)(2,1)} %copy.62) | copy-start | bytes 3456004
  247.7 10.8 %copy-start.41 = (bf16[6,64,1500]{2,1,0:T(8,128)(2,1)}, bf16[6,64,1500]{2,1,0:T(8,128)(2,1)S(1)}, u32[]{:S(2)}) copy-start(bf16[6,64,1500]{2,1,0:T(8,128)(2,1)S(1)} %convolution_convert_fusion.2) | copy-start | bytes 3456004
  248.9 5.9 %collective-permute-start.27 = (f32[384,384]{1,0:T(8,128)S(1)}, f32[384,384]{1,0:T(8,128)S(1)}, u32[]{:S(2)}, u32[]{:S(2)}) collective-permute-start(f32[384,384]{1,0:T(8,128)S(1)} %fusion.97), channel_id=1, source_target_pairs={{0,2},{2,0},{4,6},{6,4},{8,10},{10,8},{12,14},{14,12},{16,18},{18,... | collective-permute-start | bytes 1769480 | tf_op jit(solution)/shard_map/ppermute | solution.py:79
  250.3 6.5 %collective-permute-start.19 = (f32[384,384]{1,0:T(8,128)S(1)}, f32[384,384]{1,0:T(8,128)S(1)}, u32[]{:S(2)}, u32[]{:S(2)}) collective-permute-start(f32[384,384]{1,0:T(8,128)S(1)} %fusion.100), channel_id=1, source_target_pairs={{0,2},{2,0},{4,6},{6,4},{8,10},{10,8},{12,14},{14,12},{16,18},{18,... | collective-permute-start | bytes 1769480 | tf_op jit(solution)/shard_map/ppermute | solution.py:79
  252.6 43.3 %collective-permute-start.23 = (f32[384,768]{1,0:T(8,128)}, f32[384,768]{1,0:T(8,128)}, u32[]{:S(2)}, u32[]{:S(2)}) collective-permute-start(f32[384,768]{1,0:T(8,128)} %fusion.68), channel_id=1, source_target_pairs={{0,2},{2,0},{4,6},{6,4},{8,10},{10,8},{12,14},{14,12},{16,18},{18,... | collective-permute-start | bytes 3538952 | tf_op jit(solution)/shard_map/ppermute | solution.py:79
  255.9 10.1 %collective-permute-start.28 = (f32[192,384]{1,0:T(8,128)}, f32[192,384]{1,0:T(8,128)S(1)}, u32[]{:S(2)}, u32[]{:S(2)}) collective-permute-start(f32[192,384]{1,0:T(8,128)} %slice.414), channel_id=1, source_target_pairs={{0,4},{2,6},{4,0},{6,2},{8,12},{10,14},{12,8},{14,10},{16,20},{18,... | collective-permute-start | bytes 884744 | tf_op jit(solution)/shard_map/ppermute | solution.py:79
  257.3 14.2 %collective-permute-start.20 = (f32[192,384]{1,0:T(8,128)S(1)}, f32[192,384]{1,0:T(8,128)S(1)}, u32[]{:S(2)}, u32[]{:S(2)}) collective-permute-start(f32[192,384]{1,0:T(8,128)S(1)} %slice.396), channel_id=1, source_target_pairs={{0,4},{2,6},{4,0},{6,2},{8,12},{10,14},{12,8},{14,10},{16,20},{18,... | collective-permute-start | bytes 884744 | tf_op jit(solution)/shard_map/ppermute | solution.py:79
  266.0 35.0 %collective-permute-start.4 = (f32[448,768]{1,0:T(8,128)}, f32[448,768]{1,0:T(8,128)S(1)}, u32[]{:S(2)}, u32[]{:S(2)}) collective-permute-start(f32[448,768]{1,0:T(8,128)} %fusion.156), channel_id=1, source_target_pairs={{0,1},{1,0},{2,3},{3,2},{4,5},{5,4},{6,7},{7,6},{8,9},{9,8},{10,11... | collective-permute-start | bytes 4128776 | tf_op jit(solution)/shard_map/ppermute | solution.py:75
  271.4 113.0 %collective-permute-start.6 = (f32[1500,384]{1,0:T(8,128)}, f32[1500,384]{1,0:T(8,128)}, u32[]{:S(2)}, u32[]{:S(2)}) collective-permute-start(f32[1500,384]{1,0:T(8,128)} %fusion.88), channel_id=1, source_target_pairs={{0,1},{1,0},{2,3},{3,2},{4,5},{5,4},{6,7},{7,6},{8,9},{9,8},{10,11... | collective-permute-start | bytes 6912008 | tf_op jit(solution)/shard_map/ppermute | solution.py:75
  272.3 10.4 %collective-permute-start.29 = (f32[96,384]{1,0:T(8,128)S(1)}, f32[96,384]{1,0:T(8,128)S(1)}, u32[]{:S(2)}, u32[]{:S(2)}) collective-permute-start(f32[96,384]{1,0:T(8,128)S(1)} %slice.416), channel_id=1, source_target_pairs={{0,8},{2,10},{4,12},{6,14},{8,0},{10,2},{12,4},{14,6},{16,24},{18,... | collective-permute-start | bytes 442376 | tf_op jit(solution)/shard_map/ppermute | solution.py:79
  277.0 7.2 %collective-permute-start.21 = (f32[96,384]{1,0:T(8,128)S(1)}, f32[96,384]{1,0:T(8,128)S(1)}, u32[]{:S(2)}, u32[]{:S(2)}) collective-permute-start(f32[96,384]{1,0:T(8,128)S(1)} %slice.398), channel_id=1, source_target_pairs={{0,8},{2,10},{4,12},{6,14},{8,0},{10,2},{12,4},{14,6},{16,24},{18,... | collective-permute-start | bytes 442376 | tf_op jit(solution)/shard_map/ppermute | solution.py:79
  280.3 15.7 %copy-start.105 = (bf16[1500,768]{1,0:T(8,128)(2,1)S(1)}, bf16[1500,768]{1,0:T(8,128)(2,1)}, u32[]{:S(2)}) copy-start(bf16[1500,768]{1,0:T(8,128)(2,1)} %fusion.3) | copy-start | bytes 6912004
  281.3 14.6 %copy-start.48 = (bf16[6,64,1500]{2,1,0:T(8,128)(2,1)S(1)}, bf16[6,64,1500]{2,1,0:T(8,128)(2,1)}, u32[]{:S(2)}) copy-start(bf16[6,64,1500]{2,1,0:T(8,128)(2,1)} %copy-done.47) | copy-start | bytes 3456004
  282.7 13.3 %copy-start.42 = (bf16[6,64,1500]{2,1,0:T(8,128)(2,1)S(1)}, bf16[6,64,1500]{2,1,0:T(8,128)(2,1)}, u32[]{:S(2)}) copy-start(bf16[6,64,1500]{2,1,0:T(8,128)(2,1)} %copy-done.41) | copy-start | bytes 3456004
  282.7 72.8 %collective-permute-start.32 = (f32[192,1536]{1,0:T(8,128)}, f32[192,1536]{1,0:T(8,128)}, u32[]{:S(2)}, u32[]{:S(2)}) collective-permute-start(f32[192,1536]{1,0:T(8,128)} %slice.422), channel_id=1, source_target_pairs={{0,4},{2,6},{4,0},{6,2},{8,12},{10,14},{12,8},{14,10},{16,20},{18,... | collective-permute-start | bytes 3538952 | tf_op jit(solution)/shard_map/ppermute | solution.py:79
  284.2 5.3 %collective-permute-start.30 = (f32[48,384]{1,0:T(8,128)S(1)}, f32[48,384]{1,0:T(8,128)S(1)}, u32[]{:S(2)}, u32[]{:S(2)}) collective-permute-start(f32[48,384]{1,0:T(8,128)S(1)} %slice.418), channel_id=1, source_target_pairs={{0,16},{2,18},{4,20},{6,22},{8,24},{10,26},{12,28},{14,30},{16,0},... | collective-permute-start | bytes 221192 | tf_op jit(solution)/shard_map/ppermute | solution.py:79
  289.5 5.3 %collective-permute-start.22 = (f32[48,384]{1,0:T(8,128)S(1)}, f32[48,384]{1,0:T(8,128)S(1)}, u32[]{:S(2)}, u32[]{:S(2)}) collective-permute-start(f32[48,384]{1,0:T(8,128)S(1)} %slice.400), channel_id=1, source_target_pairs={{0,16},{2,18},{4,20},{6,22},{8,24},{10,26},{12,28},{14,30},{16,0},... | collective-permute-start | bytes 221192 | tf_op jit(solution)/shard_map/ppermute | solution.py:79
  294.8 63.7 %collective-permute-start.36 = (f32[192,1536]{1,0:T(8,128)}, f32[192,1536]{1,0:T(8,128)}, u32[]{:S(2)}, u32[]{:S(2)}) collective-permute-start(f32[192,1536]{1,0:T(8,128)} %slice.431), channel_id=1, source_target_pairs={{0,4},{2,6},{4,0},{6,2},{8,12},{10,14},{12,8},{14,10},{16,20},{18,... | collective-permute-start | bytes 3538952 | tf_op jit(solution)/shard_map/ppermute | solution.py:79
  299.5 47.9 %collective-permute-start.24 = (f32[192,768]{1,0:T(8,128)}, f32[192,768]{1,0:T(8,128)}, u32[]{:S(2)}, u32[]{:S(2)}) collective-permute-start(f32[192,768]{1,0:T(8,128)} %slice.404), channel_id=1, source_target_pairs={{0,4},{2,6},{4,0},{6,2},{8,12},{10,14},{12,8},{14,10},{16,20},{18,... | collective-permute-start | bytes 1769480 | tf_op jit(solution)/shard_map/ppermute | solution.py:79
  308.4 9.4 %slice-start = ((s8[5505024]{0:T(1024)(128)(4,1)}), s8[4194304]{0:T(1024)(128)(4,1)S(1)}, s32[]{:S(2)}) async-start(s8[5505024]{0:T(1024)(128)(4,1)} %bitcast.159), calls=%async_computation | async-start | bytes 8388608
  323.8 25.9 %collective-permute-start.15 = (f32[384,384]{1,0:T(8,128)}, f32[384,384]{1,0:T(8,128)}, u32[]{:S(2)}, u32[]{:S(2)}) collective-permute-start(f32[384,384]{1,0:T(8,128)} %fusion.103), channel_id=1, source_target_pairs={{0,2},{2,0},{4,6},{6,4},{8,10},{10,8},{12,14},{14,12},{16,18},{18,... | collective-permute-start | bytes 1769480 | tf_op jit(solution)/shard_map/ppermute | solution.py:79
  327.9 19.5 %copy-start.50 = (f32[384,768]{1,0:T(8,128)S(1)}, f32[384,768]{1,0:T(8,128)}, u32[]{:S(2)}) copy-start(f32[384,768]{1,0:T(8,128)} %copy-done.49) | copy-start | bytes 3538948
  329.8 20.5 %copy-start.57 = (bf16[448,768]{1,0:T(8,128)(2,1)S(1)}, bf16[448,768]{1,0:T(8,128)(2,1)}, u32[]{:S(2)}) copy-start(bf16[448,768]{1,0:T(8,128)(2,1)} %fusion.49) | copy-start | bytes 2064388
  348.6 6.8 %collective-permute-start.25 = (f32[96,768]{1,0:T(8,128)S(1)}, f32[96,768]{1,0:T(8,128)S(1)}, u32[]{:S(2)}, u32[]{:S(2)}) collective-permute-start(f32[96,768]{1,0:T(8,128)S(1)} %slice.406), channel_id=1, source_target_pairs={{0,8},{2,10},{4,12},{6,14},{8,0},{10,2},{12,4},{14,6},{16,24},{18,... | collective-permute-start | bytes 884744 | tf_op jit(solution)/shard_map/ppermute | solution.py:79
  349.7 51.4 %collective-permute-start.5 = (f32[448,768]{1,0:T(8,128)}, f32[448,768]{1,0:T(8,128)}, u32[]{:S(2)}, u32[]{:S(2)}) collective-permute-start(f32[448,768]{1,0:T(8,128)} %fusion.136), channel_id=1, source_target_pairs={{0,1},{1,0},{2,3},{3,2},{4,5},{5,4},{6,7},{7,6},{8,9},{9,8},{10,11... | collective-permute-start | bytes 4128776 | tf_op jit(solution)/shard_map/ppermute | solution.py:75
  355.4 81.8 %collective-permute-start.7 = (f32[384,1152]{1,0:T(8,128)}, f32[384,1152]{1,0:T(8,128)}, u32[]{:S(2)}, u32[]{:S(2)}) collective-permute-start(f32[384,1152]{1,0:T(8,128)} %fusion.106), channel_id=1, source_target_pairs={{0,2},{2,0},{4,6},{6,4},{8,10},{10,8},{12,14},{14,12},{16,18},{18,... | collective-permute-start | bytes 5308424 | tf_op jit(solution)/shard_map/ppermute | solution.py:79
  355.5 9.5 %collective-permute-start.16 = (f32[192,384]{1,0:T(8,128)S(1)}, f32[192,384]{1,0:T(8,128)S(1)}, u32[]{:S(2)}, u32[]{:S(2)}) collective-permute-start(f32[192,384]{1,0:T(8,128)S(1)} %slice.388), channel_id=1, source_target_pairs={{0,4},{2,6},{4,0},{6,2},{8,12},{10,14},{12,8},{14,10},{16,20},{18,... | collective-permute-start | bytes 884744 | tf_op jit(solution)/shard_map/ppermute | solution.py:79
  358.5 10.2 %collective-permute-start.26 = (f32[48,768]{1,0:T(8,128)S(1)}, f32[48,768]{1,0:T(8,128)S(1)}, u32[]{:S(2)}, u32[]{:S(2)}) collective-permute-start(f32[48,768]{1,0:T(8,128)S(1)} %slice.408), channel_id=1, source_target_pairs={{0,16},{2,18},{4,20},{6,22},{8,24},{10,26},{12,28},{14,30},{16,0},... | collective-permute-start | bytes 442376 | tf_op jit(solution)/shard_map/ppermute | solution.py:79
  365.0 47.8 %collective-permute-start.33 = (f32[96,1536]{1,0:T(8,128)}, f32[96,1536]{1,0:T(8,128)}, u32[]{:S(2)}, u32[]{:S(2)}) collective-permute-start(f32[96,1536]{1,0:T(8,128)} %slice.424), channel_id=1, source_target_pairs={{0,8},{2,10},{4,12},{6,14},{8,0},{10,2},{12,4},{14,6},{16,24},{18,... | collective-permute-start | bytes 1769480 | tf_op jit(solution)/shard_map/ppermute | solution.py:79
  368.7 15.7 %collective-permute-start.17 = (f32[96,384]{1,0:T(8,128)}, f32[96,384]{1,0:T(8,128)S(1)}, u32[]{:S(2)}, u32[]{:S(2)}) collective-permute-start(f32[96,384]{1,0:T(8,128)} %slice.390), channel_id=1, source_target_pairs={{0,8},{2,10},{4,12},{6,14},{8,0},{10,2},{12,4},{14,6},{16,24},{18,... | collective-permute-start | bytes 442376 | tf_op jit(solution)/shard_map/ppermute | solution.py:79
  384.4 32.6 %collective-permute-start.37 = (f32[96,1536]{1,0:T(8,128)}, f32[96,1536]{1,0:T(8,128)S(1)}, u32[]{:S(2)}, u32[]{:S(2)}) collective-permute-start(f32[96,1536]{1,0:T(8,128)} %slice.433), channel_id=1, source_target_pairs={{0,8},{2,10},{4,12},{6,14},{8,0},{10,2},{12,4},{14,6},{16,24},{18,... | collective-permute-start | bytes 1769480 | tf_op jit(solution)/shard_map/ppermute | solution.py:79
  384.4 16.0 %collective-permute-start.18 = (f32[48,384]{1,0:T(8,128)S(1)}, f32[48,384]{1,0:T(8,128)S(1)}, u32[]{:S(2)}, u32[]{:S(2)}) collective-permute-start(f32[48,384]{1,0:T(8,128)S(1)} %slice.392), channel_id=1, source_target_pairs={{0,16},{2,18},{4,20},{6,22},{8,24},{10,26},{12,28},{14,30},{16,0},... | collective-permute-start | bytes 221192 | tf_op jit(solution)/shard_map/ppermute | solution.py:79
  404.3 1.3 collective-permute-start.11
  405.6 4.2 collective-permute-start.12
  407.9 9.2 %copy-start.28 = (f32[192,1536]{1,0:T(8,128)S(1)}, f32[192,1536]{1,0:T(8,128)}, u32[]{:S(2)}) copy-start(f32[192,1536]{1,0:T(8,128)} %copy-done.27) | copy-start | bytes 3538948
  409.8 5.0 %collective-permute-start.13 = (f32[11520]{0:T(1024)S(1)}, f32[11520]{0:T(1024)S(1)}, u32[]{:S(2)}, u32[]{:S(2)}) collective-permute-start(f32[11520]{0:T(1024)S(1)} %add.431), channel_id=1, source_target_pairs={{0,8},{2,10},{4,12},{6,14},{8,0},{10,2},{12,4},{14,6},{16,24},{18,... | collective-permute-start | bytes 138248 | tf_op jit(solution)/shard_map/ppermute | solution.py:79
  413.9 23.2 %copy-start.46 = (bf16[6,64,448]{2,1,0:T(8,128)(2,1)S(1)}, bf16[6,64,448]{2,1,0:T(8,128)(2,1)}, u32[]{:S(2)}) copy-start(bf16[6,64,448]{2,1,0:T(8,128)(2,1)} %copy-done.45) | copy-start | bytes 1032196
  413.9 23.2 %copy-start.64 = (bf16[6,64,448]{2,1,0:T(8,128)(2,1)S(1)}, bf16[6,64,448]{2,1,0:T(8,128)(2,1)}, u32[]{:S(2)}) copy-start(bf16[6,64,448]{2,1,0:T(8,128)(2,1)} %get-tuple-element.128) | copy-start | bytes 1032196
  414.0 23.2 %copy-start.66 = (bf16[448,768]{1,0:T(8,128)(2,1)S(1)}, bf16[448,768]{1,0:T(8,128)(2,1)}, u32[]{:S(2)}) copy-start(bf16[448,768]{1,0:T(8,128)(2,1)} %fusion.48) | copy-start | bytes 2064388
  414.0 47.3 %collective-permute-start.34 = (f32[48,1536]{1,0:T(8,128)S(1)}, f32[48,1536]{1,0:T(8,128)S(1)}, u32[]{:S(2)}, u32[]{:S(2)}) collective-permute-start(f32[48,1536]{1,0:T(8,128)S(1)} %slice.426), channel_id=1, source_target_pairs={{0,16},{2,18},{4,20},{6,22},{8,24},{10,26},{12,28},{14,30},{16,0},... | collective-permute-start | bytes 884744 | tf_op jit(solution)/shard_map/ppermute | solution.py:79
  414.8 22.3 %collective-permute-start.14 = (f32[11520]{0:T(1024)S(1)}, f32[11520]{0:T(1024)S(1)}, u32[]{:S(2)}, u32[]{:S(2)}) collective-permute-start(f32[11520]{0:T(1024)S(1)} %add.432), channel_id=1, source_target_pairs={{0,16},{2,18},{4,20},{6,22},{8,24},{10,26},{12,28},{14,30},{16,0},... | collective-permute-start | bytes 138248 | tf_op jit(solution)/shard_map/ppermute | solution.py:79
  417.2 55.4 %collective-permute-start.38 = (f32[48,1536]{1,0:T(8,128)S(1)}, f32[48,1536]{1,0:T(8,128)S(1)}, u32[]{:S(2)}, u32[]{:S(2)}) collective-permute-start(f32[48,1536]{1,0:T(8,128)S(1)} %slice.435), channel_id=1, source_target_pairs={{0,16},{2,18},{4,20},{6,22},{8,24},{10,26},{12,28},{14,30},{16,0},... | collective-permute-start | bytes 884744 | tf_op jit(solution)/shard_map/ppermute | solution.py:79
  439.5 21.5 %collective-permute-start.8 = (f32[192,1152]{1,0:T(8,128)S(1)}, f32[192,1152]{1,0:T(8,128)S(1)}, u32[]{:S(2)}, u32[]{:S(2)}) collective-permute-start(f32[192,1152]{1,0:T(8,128)S(1)} %slice.378), channel_id=1, source_target_pairs={{0,4},{2,6},{4,0},{6,2},{8,12},{10,14},{12,8},{14,10},{16,20},{18,... | collective-permute-start | bytes 2654216 | tf_op jit(solution)/shard_map/ppermute | solution.py:79
  461.2 11.2 %collective-permute-start.9 = (f32[96,1152]{1,0:T(8,128)S(1)}, f32[96,1152]{1,0:T(8,128)S(1)}, u32[]{:S(2)}, u32[]{:S(2)}) collective-permute-start(f32[96,1152]{1,0:T(8,128)S(1)} %slice.380), channel_id=1, source_target_pairs={{0,8},{2,10},{4,12},{6,14},{8,0},{10,2},{12,4},{14,6},{16,24},{18,... | collective-permute-start | bytes 1327112 | tf_op jit(solution)/shard_map/ppermute | solution.py:79
  472.4 12.0 %copy-start.1 = (bf16[768,1536]{1,0:T(8,128)(2,1)S(1)}, bf16[768,1536]{1,0:T(8,128)(2,1)}, u32[]{:S(2)}) copy-start(bf16[768,1536]{1,0:T(8,128)(2,1)} %param.28) | copy-start | bytes 7077892
  472.5 11.2 %collective-permute-start.10 = (f32[48,1152]{1,0:T(8,128)S(1)}, f32[48,1152]{1,0:T(8,128)S(1)}, u32[]{:S(2)}, u32[]{:S(2)}) collective-permute-start(f32[48,1152]{1,0:T(8,128)S(1)} %slice.382), channel_id=1, source_target_pairs={{0,16},{2,18},{4,20},{6,22},{8,24},{10,26},{12,28},{14,30},{16,0},... | collective-permute-start | bytes 663560 | tf_op jit(solution)/shard_map/ppermute | solution.py:79
  (85 other events, 271.9 us)
